TPU v7x, 256 devices: a whole 4x4x8 slice. The times are simulated.
256 devices in a mesh: circ: 64 (over z, y_hi, x), ax: 4 (over y_lo, core).
Axes of the slice: x: 4, y: 4 (y_hi: 2, y_lo: 2; y = y_hi * 2 + y_lo), z: 8, core: 2. Of those that a mesh axis runs over, the one named last changes fastest.
Arguments:
- fields: float32 [3, 8, 512, 1024], P(None, None, 'circ', 'ax'), may hold values from -6 to 6
Outputs:
- deriv_circ: float32 [3, 8, 512, 1024], P(None, None, 'circ', 'ax')
- deriv_axial: float32 [3, 8, 512, 1024], P(None, None, 'circ', 'ax')
- filtered: float32 [3, 8, 512, 1024], P(None, None, 'circ', 'ax')
All inputs are finite; a program needn't handle non-finite values.
Results may differ from a plain program's by a relative error of at most 0.0003.
Values sent between devices are 32-bit elements; how exact they have to be, the bound alone decides.
No kernel may reach another device: no remote copies, remote signals or barrier semaphores. Data moves between devices by JAX's collectives and lax.ppermute only.
A program may use at most 64 MiB of HBM per device.

v0:
```python
import math
import jax
import jax.numpy as jnp
import numpy as np
from jax import lax
from jax.sharding import PartitionSpec as P

DERIV_NEAR = 14.0 / 9.0
DERIV_FAR = 1.0 / 9.0
ALPHA_DERIV = 1.0 / 3.0
ALPHA_FILTER = 0.4999
PRECISE = lax.Precision.HIGHEST


def with_halo(value, sides, width, wrap):
    for axis, dim in sides:
        peers, length = (lax.axis_size(axis), value.shape[dim])
        up = [(i, (i + 1) % peers) for i in range(peers if wrap else peers - 1)]
        down = [(j, i) for i, j in up]
        last = lax.slice_in_dim(value, length - width, length, axis=dim)
        initial = lax.slice_in_dim(value, 0, width, axis=dim)
        before = lax.ppermute(last, axis, up)
        after = lax.ppermute(initial, axis, down)
        value = jnp.concatenate([before, value, after], axis=dim)
    return value


def entering_2(part, axis, combine, identity, reverse):
    count = lax.axis_size(axis)
    place = lax.axis_index(axis)
    ahead = count - 1 - place if reverse else place
    gathered = jax.tree.map(lambda a: lax.all_gather(a, axis), part)
    state = jax.tree.map(lambda a, e: jnp.zeros_like(a) + jnp.asarray(e, a.dtype), part, identity)

    def one(step, state):
        source = count - 1 - step if reverse else step
        return combine(
            state, jax.tree.map(lambda a: lax.dynamic_index_in_dim(a, source, 0, False), gathered)
        )

    return lax.fori_loop(0, ahead, one, state)


def filter_terms(coupling):
    return [
        (193.0 + 126.0 * coupling) / 256.0,
        (105.0 + 302.0 * coupling) / 256.0,
        15.0 * (2.0 * coupling - 1.0) / 64.0,
        45.0 * (1.0 - 2.0 * coupling) / 512.0,
        5.0 * (2.0 * coupling - 1.0) / 256.0,
        (1.0 - 2.0 * coupling) / 512.0,
    ]


def root_of(coupling):
    return (-1.0 + math.sqrt(1.0 - 4.0 * coupling * coupling)) / (2.0 * coupling)


def signed_power(exponent, log_sizes):
    magnitude = jnp.exp(exponent[..., None].astype(jnp.float32) * log_sizes)
    parity = (exponent % 2).astype(jnp.float32)
    return magnitude * (1.0 - 2.0 * parity)[..., None]


def affine_chain(earlier, later):
    return (earlier[0] * later[0], later[0] * earlier[1] + later[1])


def running_products(values):
    result = np.zeros(len(values))
    running = 1.0
    for place in range(len(values)):
        running = running * values[place]
        result[place] = running
    return result


def axial_rhs(shifted, row_index, line_length):
    interior = 0.5 * DERIV_NEAR * (shifted(1) - shifted(-1)) + 0.25 * DERIV_FAR * (
        shifted(2) - shifted(-2)
    )
    row_opening = -2.5 * shifted(0) + 2.0 * shifted(1) + 0.5 * shifted(2)
    row_second = 0.75 * (shifted(1) - shifted(-1))
    row_closing = 2.5 * shifted(0) - 2.0 * shifted(-1) - 0.5 * shifted(-2)
    result = jnp.where(row_index == 0, row_opening, interior)
    result = jnp.where((row_index == 1) | (row_index == line_length - 2), row_second, result)
    return jnp.where(row_index == line_length - 1, row_closing, result)


def bands_table(line_length):
    band_lower = np.full(line_length, ALPHA_DERIV)
    band_lower[0] = 0.0
    band_lower[1] = 0.25
    band_lower[line_length - 2] = 0.25
    band_lower[line_length - 1] = 2.0
    band_middle = np.ones(line_length)
    band_upper = np.full(line_length, ALPHA_DERIV)
    band_upper[0] = 2.0
    band_upper[1] = 0.25
    band_upper[line_length - 2] = 0.25
    band_upper[line_length - 1] = 0.0
    return (band_lower, band_middle, band_upper)


def thomas_tables(line_cells, axial_count):
    line_length = line_cells * axial_count
    band_lower, band_middle, band_upper = bands_table(line_length)
    pivots = np.zeros(line_length)
    factors = np.zeros(line_length)
    pivots[0] = band_middle[0]
    for row_number in range(1, line_length):
        factors[row_number] = -band_lower[row_number] / pivots[row_number - 1]
        pivots[row_number] = (
            band_middle[row_number] + factors[row_number] * band_upper[row_number - 1]
        )
    backs = -band_upper / pivots
    fwd_blocks, fwd_grows, back_blocks, back_grows, inv_pivots = ([], [], [], [], [])
    for place in range(axial_count):
        base_row = place * line_cells
        seg_fwd = factors[base_row : base_row + line_cells]
        seg_back = backs[base_row : base_row + line_cells]
        block_fwd = np.zeros((line_cells, line_cells))
        block_back = np.zeros((line_cells, line_cells))
        for target in range(line_cells):
            running = 1.0
            block_fwd[target, target] = 1.0
            for source in range(target - 1, -1, -1):
                running = running * seg_fwd[source + 1]
                block_fwd[target, source] = running
            running = 1.0
            block_back[target, target] = 1.0
            for source in range(target + 1, line_cells):
                running = running * seg_back[source - 1]
                block_back[target, source] = running
        fwd_blocks.append(block_fwd)
        fwd_grows.append(running_products(seg_fwd))
        back_blocks.append(block_back)
        back_grows.append(running_products(seg_back[::-1])[::-1])
        inv_pivots.append(1.0 / pivots[base_row : base_row + line_cells])
    return [
        jnp.asarray(np.stack(table), jnp.float32)
        for table in (fwd_blocks, fwd_grows, back_blocks, back_grows, inv_pivots)
    ]


def shards(fields):
    cells = fields.shape[2]
    line_cells = fields.shape[3]
    roots = [root_of(ALPHA_DERIV), root_of(ALPHA_FILTER)]
    circ_count = lax.axis_size("circ")
    circ_place = lax.axis_index("circ")
    loop_cells = cells * circ_count
    log_sizes = jnp.asarray([math.log(abs(root_value)) for root_value in roots], jnp.float32)
    wrap_scale = jnp.asarray(
        [1.0 / (1.0 - root_value**loop_cells) for root_value in roots], jnp.float32
    )
    padded = with_halo(fields, (("circ", 2),), 5, True)

    def circ_take(offset):
        return padded[:, :, 5 + offset : 5 + offset + cells, :]

    circ_right = 0.5 * DERIV_NEAR * (circ_take(1) - circ_take(-1)) + 0.25 * DERIV_FAR * (
        circ_take(2) - circ_take(-2)
    )
    terms = filter_terms(ALPHA_FILTER)
    filter_right = terms[0] * circ_take(0)
    for offset in range(1, 6):
        filter_right = filter_right + 0.5 * terms[offset] * (circ_take(offset) + circ_take(-offset))
    scaled = jnp.stack([circ_right * (1.0 + roots[0] ** 2), filter_right * (1.0 + roots[1] ** 2)])
    cell_steps = np.arange(cells)
    cell_gap = cell_steps[:, None] - cell_steps[None, :]
    forward_np = np.stack(
        [
            np.where(cell_gap >= 0, root_value ** np.maximum(cell_gap, 0), 0.0)
            for root_value in roots
        ]
    )
    backward_np = np.stack(
        [
            np.where(cell_gap <= 0, root_value ** np.maximum(-cell_gap, 0), 0.0)
            for root_value in roots
        ]
    )
    forward_table = jnp.asarray(forward_np, jnp.float32)
    backward_table = jnp.asarray(backward_np, jnp.float32)
    grow_forward = jnp.asarray(
        np.stack([root_value ** (cell_steps + 1) for root_value in roots]), jnp.float32
    )
    grow_backward = jnp.asarray(
        np.stack([root_value ** (cells - cell_steps) for root_value in roots]), jnp.float32
    )

    def circ_carry(state, backward):
        piece = lax.all_gather(state[None], "circ", axis=0, tiled=True)
        shard_ids = jnp.arange(piece.shape[0], dtype=jnp.int32)
        if backward:
            distance = (shard_ids - circ_place - 1) % circ_count
        else:
            distance = (circ_place - shard_ids - 1) % circ_count
        weights = signed_power(distance * cells, log_sizes) * wrap_scale
        return jnp.zeros_like(state) + jnp.einsum(
            "qs,qsfna->sfna", weights, piece, precision=PRECISE
        )

    partial_forward = jnp.einsum("sjk,sfnka->sfnja", forward_table, scaled, precision=PRECISE)
    incoming = circ_carry(partial_forward[:, :, :, -1, :], False)
    forward_full = (
        partial_forward + grow_forward[:, None, None, :, None] * incoming[:, :, :, None, :]
    )
    partial_back = jnp.einsum("sjk,sfnka->sfnja", backward_table, forward_full, precision=PRECISE)
    incoming_back = circ_carry(partial_back[:, :, :, 0, :], True)
    solved = partial_back + grow_backward[:, None, None, :, None] * incoming_back[:, :, :, None, :]
    deriv_circ = solved[0]
    filtered = solved[1]
    axial_count = lax.axis_size("ax")
    axial_place = lax.axis_index("ax")
    line_length = line_cells * axial_count
    padded_axial = with_halo(fields, (("ax", 3),), 2, False)

    def axial_take(offset):
        return padded_axial[:, :, :, 2 + offset : 2 + offset + line_cells]

    global_rows = axial_place * line_cells + jnp.arange(line_cells, dtype=jnp.int32)
    axial_right = axial_rhs(axial_take, global_rows, line_length)
    tables = thomas_tables(line_cells, axial_count)
    fwd_block, fwd_grow, back_block, back_grow, inv_pivot = [
        lax.dynamic_index_in_dim(table, axial_place, 0, keepdims=False) for table in tables
    ]

    def axial_carry(multiplier, state, backward):
        identity = (jnp.ones_like(multiplier), jnp.zeros_like(state))
        return entering_2((multiplier, state), "ax", affine_chain, identity, backward)[1]

    local_fwd = jnp.einsum("fnck,jk->fncj", axial_right, fwd_block, precision=PRECISE)
    entering = axial_carry(fwd_grow[-1].reshape(1, 1, 1), local_fwd[:, :, :, -1], False)
    eliminated = (local_fwd + fwd_grow * entering[:, :, :, None]) * inv_pivot
    local_back = jnp.einsum("fnck,jk->fncj", eliminated, back_block, precision=PRECISE)
    entering_back = axial_carry(back_grow[0].reshape(1, 1, 1), local_back[:, :, :, 0], True)
    deriv_axial = local_back + back_grow * entering_back[:, :, :, None]
    return (deriv_circ, deriv_axial, filtered)


def solution(mesh):
    placed = (P(None, None, "circ", "ax"),)
    return jax.shard_map(
        shards,
        mesh=mesh,
        in_specs=placed,
        out_specs=(
            P(None, None, "circ", "ax"),
            P(None, None, "circ", "ax"),
            P(None, None, "circ", "ax"),
        ),
        check_vma=False,
    )
```

profile of v0, /device:TPU:2, one launch (start us, length us, event | category | flops | bytes accessed | tf_op | source)
XLA Modules:
  0.0 288.8 jit_solution(12185485005442516595)
XLA Ops:
  7.2 1.1 fusion.99
  8.3 2.3 collective-permute-start
  10.6 0.9 constant_dynamic-update-slice_fusion.1
  11.6 3.5 %collective-permute-done = f32[3,8,5,256]{3,2,1,0:T(8,128)S(1)} collective-permute-done((f32[3,8,5,256]{3,2,1,0:T(8,128)S(1)}, f32[3,8,5,256]{3,2,1,0:T(8,128)S(1)}, u32[]{:S(2)}, u32[]{:S(2)}) %collective-permute-start) | collective-permute-done | bytes 122912 | tf_op jit(solution)/shard_map/ppermute | solution.py:23
  15.1 9.1 %collective-permute-done.1 = f32[3,8,5,256]{3,2,1,0:T(8,128)S(1)} collective-permute-done((f32[3,8,5,256]{3,2,1,0:T(8,128)S(1)}, f32[3,8,5,256]{3,2,1,0:T(8,128)S(1)}, u32[]{:S(2)}, u32[]{:S(2)}) %collective-permute-start.1) | collective-permute-done | bytes 122912 | tf_op jit(solution)/shard_map/ppermute | solution.py:22
  24.2 2.5 multiply_bitcast_fusion
  28.1 121.8 %all-gather.9.cloned.1.call-done = f32[128,3,8,1,256]{4,2,3,1,0:T(8,128)} async-done(((f32[2,3,8,1,256]{4,2,3,1,0:T(8,128)}), f32[128,3,8,1,256]{4,2,3,1,0:T(8,128)}) %all-gather.9.cloned.1.call-update) | async-done | bytes 3145744 | tf_op jit(solution)/shard_map/all_gather | solution.py:194
  150.0 5.1 %fusion.2 = f32[2,1,3,8,256]{4,1,3,2,0:T(1,128)S(1)} fusion(f32[64,2,1,1,1]{0,2,4,3,1:T(1,128)S(1)} %bitcast.83, f32[64,2,3,8,256]{4,3,2,1,0:T(8,128)} %bitcast.77), kind=kOutput, calls=%fused_computation.6 | convolution fusion | flops 9437184 | bytes 3195392 | tf_op jit(solution)/shard_map/qs,qsfna->sfna/dot_general | solution.py:201
  156.4 1.3 collective-permute-start.3
  157.7 3.0 %collective-permute-start.2 = (f32[3,8,8,2]{3,2,1,0:T(8,128)S(1)}, f32[3,8,8,2]{3,2,1,0:T(8,128)S(1)}, u32[]{:S(2)}, u32[]{:S(2)}) collective-permute-start(f32[3,8,8,2]{3,2,1,0:T(8,128)S(1)} %get-tuple-element.159), channel_id=1, source_target_pairs={{0,1},{1,2},{2,3},{4,5},{5,6},{6,7},{8,9},{9,10},{10,11},{12,13},{... | collective-permute-start | bytes 4616 | tf_op jit(solution)/shard_map/ppermute | solution.py:22
  161.4 1.3 dynamic-slice.2
  162.7 1.3 bitcast_dynamic-update-slice_fusion.1
  164.0 1.4 bitcast_dynamic-update-slice_fusion
  166.1 0.7 constant_dynamic-slice_fusion.3
  166.8 6.3 %all-reduce.2 = (f32[4]{0:T(128)S(1)}, f32[4]{0:T(128)S(1)}) all-reduce(f32[4]{0:T(128)S(1)} %bitcast_dynamic-update-slice_fusion.1, f32[4]{0:T(128)S(1)} %bitcast_dynamic-update-slice_fusion), channel_id=4, replica_groups=mesh['circ'=64,'ax'=4] {'ax'}, use_global_device_ids=true, to_apply=%add | all-reduce | flops 8 | bytes 64
  173.1 1.5 fusion.11
  175.0 5.2 %all-gather.3 = f32[12,8,8,1]{2,1,3,0:T(8,128)S(1)} all-gather(f32[3,8,8,1]{2,1,3,0:T(8,128)S(1)} %copy.21), channel_id=5, replica_groups=mesh['circ'=64,'ax'=4] {'ax'}, dimensions={0}, use_global_device_ids=true | all-gather | bytes 3840 | tf_op jit(solution)/shard_map/all_gather | solution.py:32
  180.2 1.4 fusion.9
  181.8 8.7 %all-gather.5 = f32[12,8,8,1]{2,1,3,0:T(8,128)S(1)} all-gather(f32[3,8,8,1]{2,1,3,0:T(8,128)S(1)} %copy.22), channel_id=7, replica_groups=mesh['circ'=64,'ax'=4] {'ax'}, dimensions={0}, use_global_device_ids=true | all-gather | bytes 3840 | tf_op jit(solution)/shard_map/all_gather | solution.py:32
  190.5 4.0 %while.27 = (s32[]{:T(128)}, f32[3,8,8]{2,1,0:T(8,128)S(1)}, s32[]{:T(128)}, f32[4,1,1,1]{0,3,2,1:T(1,128)S(1)}, f32[4,3,8,8]{3,2,1,0:T(8,128)S(1)}, /*index=5*/s32[]{:T(128)}, s32[]{:T(128)}, s32[]{:T(128)}, s32[]{:T(128)}) while((s32[]{:T(128)}, f32[3,8,8]{2,1,0:T(8,128)S(1)}, s32[]{:T(128)}, f32[4,1,1,1]{0,3,2,1:T(1,128)S(1)}, ...), condition=%wide.region_3.4_spmd, body=%wide.region_2.3_spmd.sunk | while | flops 390 | bytes 2463 | solution.py:41
  194.5 0.8 multiply_add_fusion.1
  195.3 80.7 %all-gather.11.cloned.1.call-done = f32[128,3,8,1,256]{4,2,3,1,0:T(8,128)} async-done(((f32[2,3,8,1,256]{4,2,3,1,0:T(8,128)}), f32[128,3,8,1,256]{4,2,3,1,0:T(8,128)}) %all-gather.11.cloned.1.call-update) | async-done | bytes 3145744 | tf_op jit(solution)/shard_map/all_gather | solution.py:194
  276.0 5.1 %fusion = f32[2,1,3,8,256]{4,1,3,2,0:T(1,128)S(1)} fusion(f32[64,2,1,1,1]{0,2,4,3,1:T(1,128)S(1)} %bitcast.82, f32[64,2,3,8,256]{4,3,2,1,0:T(8,128)} %bitcast.76), kind=kOutput, calls=%fused_computation.4 | convolution fusion | flops 9437184 | bytes 3195392 | tf_op jit(solution)/shard_map/qs,qsfna->sfna/dot_general | solution.py:201
  281.2 0.8 slice_bitcast_fusion
  (57 shorter events, 8.3 us)
Async XLA Ops:
  7.2 19.6 %copy-start.2 = (f32[2,8,8,1,1]{2,1,4,3,0:T(8,128)S(1)}, f32[2,8,8,1,1]{2,1,4,3,0:T(8,128)}, u32[]{:S(2)}) copy-start(f32[2,8,8,1,1]{2,1,4,3,0:T(8,128)} %constant.206) | copy-start | bytes 1540
  7.2 20.9 %copy-start.5 = (f32[2]{0:T(128)S(1)}, f32[2]{0:T(128)}, u32[]{:S(2)}) copy-start(f32[2]{0:T(128)} %constant.182.clone) | copy-start | bytes 28
  7.2 20.9 %copy-start.6 = (f32[2]{0:T(128)S(1)}, f32[2]{0:T(128)}, u32[]{:S(2)}) copy-start(f32[2]{0:T(128)} %constant.183.clone) | copy-start | bytes 28
  7.2 142.8 %all-gather.9.cloned.1.call-start = ((), (), s32[]{:S(2)}) async-start(), calls=%async_computation | async-start | bytes 3194880 | tf_op jit(solution)/shard_map/all_gather | solution.py:194
  8.3 6.7 %collective-permute-start = (f32[3,8,5,256]{3,2,1,0:T(8,128)S(1)}, f32[3,8,5,256]{3,2,1,0:T(8,128)S(1)}, u32[]{:S(2)}, u32[]{:S(2)}) collective-permute-start(f32[3,8,5,256]{3,2,1,0:T(8,128)S(1)} %get-tuple-element.162), channel_id=1, source_target_pairs={{4,0},{8,4},{12,8},{16,12},{20,16},{24,20},{28,24},{32,28},{36,32}... | collective-permute-start | bytes 368648 | tf_op jit(solution)/shard_map/ppermute | solution.py:23
  10.6 13.6 %collective-permute-start.1 = (f32[3,8,5,256]{3,2,1,0:T(8,128)S(1)}, f32[3,8,5,256]{3,2,1,0:T(8,128)S(1)}, u32[]{:S(2)}, u32[]{:S(2)}) collective-permute-start(f32[3,8,5,256]{3,2,1,0:T(8,128)S(1)} %get-tuple-element.163), channel_id=1, source_target_pairs={{0,4},{4,8},{8,12},{12,16},{16,20},{20,24},{24,28},{28,32},{32,36}... | collective-permute-start | bytes 368648 | tf_op jit(solution)/shard_map/ppermute | solution.py:22
  15.0 140.1 %copy-start.1 = (f32[2,8,8,1,1]{2,1,4,3,0:T(8,128)S(1)}, f32[2,8,8,1,1]{2,1,4,3,0:T(8,128)}, u32[]{:S(2)}) copy-start(f32[2,8,8,1,1]{2,1,4,3,0:T(8,128)} %constant.207) | copy-start | bytes 1540
  15.1 140.0 %copy-start.4 = (f32[2,8]{1,0:T(2,128)S(1)}, f32[2,8]{1,0:T(2,128)}, u32[]{:S(2)}) copy-start(f32[2,8]{1,0:T(2,128)} %constant.186.clone) | copy-start | bytes 196
  26.8 129.6 %copy-start = (f32[3,8,8,256]{3,2,1,0:T(8,128)S(1)}, f32[3,8,8,256]{3,2,1,0:T(8,128)}, u32[]{:S(2)}) copy-start(f32[3,8,8,256]{3,2,1,0:T(8,128)} %param.16) | copy-start | bytes 589828
  26.8 134.0 %copy-start.7 = (u32[256]{0:T(256)S(1)}, u32[256]{0:T(256)}, u32[]{:S(2)}) copy-start(u32[256]{0:T(256)} %constant.196) | copy-start | bytes 3076
  27.9 248.0 %all-gather.11.cloned.1.call-start = ((), (), s32[]{:S(2)}) async-start(), calls=%async_computation.1 | async-start | bytes 3194880 | tf_op jit(solution)/shard_map/all_gather | solution.py:194
  156.4 16.7 %collective-permute-start.3 = (f32[3,8,8,2]{3,2,1,0:T(8,128)S(1)}, f32[3,8,8,2]{3,2,1,0:T(8,128)S(1)}, u32[]{:S(2)}, u32[]{:S(2)}) collective-permute-start(f32[3,8,8,2]{3,2,1,0:T(8,128)S(1)} %get-tuple-element.160), channel_id=1, source_target_pairs={{1,0},{2,1},{3,2},{5,4},{6,5},{7,6},{9,8},{10,9},{11,10},{13,12},{... | collective-permute-start | bytes 4616 | tf_op jit(solution)/shard_map/ppermute | solution.py:23
  157.7 15.4 %collective-permute-start.2 = (f32[3,8,8,2]{3,2,1,0:T(8,128)S(1)}, f32[3,8,8,2]{3,2,1,0:T(8,128)S(1)}, u32[]{:S(2)}, u32[]{:S(2)}) collective-permute-start(f32[3,8,8,2]{3,2,1,0:T(8,128)S(1)} %get-tuple-element.159), channel_id=1, source_target_pairs={{0,1},{1,2},{2,3},{4,5},{5,6},{6,7},{8,9},{9,10},{10,11},{12,13},{... | collective-permute-start | bytes 4616 | tf_op jit(solution)/shard_map/ppermute | solution.py:22
  174.7 106.4 %copy-start.3 = (f32[2,8]{1,0:T(2,128)S(1)}, f32[2,8]{1,0:T(2,128)}, u32[]{:S(2)}) copy-start(f32[2,8]{1,0:T(2,128)} %constant.187.clone) | copy-start | bytes 196
Sparse Core Ops, SparseCore 0:
  28.1 121.8 all-gather.8
  156.5 119.4 all-gather.10
where the time goes:
time: 289 us
  waiting for transfers between devices  215 us (74%)
  blocking collectives  20.2 us (7%)
  between operations  14.4 us (5%)
  matrix products  14.1 us (5%)
  local copies, waits for them, and re-layouts  12.5 us (4%)
  starting transfers between devices  6.73 us (2%)
  other arithmetic  5.5 us (2%)
    all_gather x2, waiting for transfers between devices, circ_carry(): piece = lax.all_gather(state[None], 'circ', axis=0, tiled=True)  203 us
    all_gather x2, blocking collectives, entering_2(): gathered = jax.tree.map(lambda a: lax.all_gather(a, axis), part)  13.9 us
    dot_general x2, matrix products, circ_carry(): jnp.einsum('qs,qsfna->sfna', weights, piece, precision=PRECISE)  10.2 us
    ppermute x2, waiting for transfers between devices, with_halo(): before = lax.ppermute(last, axis, up)  9.15 us
    unnamed x1, blocking collectives  6.26 us
  transfers between devices with their start and end apart: 6, of which 4 were waited for; matrix products, arithmetic and copies ran while one was open for 5% of the time, Pallas kernels for 0%

commit v1 on v0

--- a/solution.py
+++ b/solution.py
@@ -191,7 +191,9 @@
     )
 
     def circ_carry(state, backward):
-        piece = lax.all_gather(state[None], "circ", axis=0, tiled=True)
+        piece = jnp.concatenate(
+            lax.all_to_all(jnp.stack([state[None]] * lax.axis_size("circ")), "circ", 0, 0), axis=0
+        )
         shard_ids = jnp.arange(piece.shape[0], dtype=jnp.int32)
         if backward:
             distance = (shard_ids - circ_place - 1) % circ_count

time: 289 us -> 200 us (0.69)
  waiting for transfers between devices: 215 us -> 96.4 us
  starting transfers between devices: 6.73 us -> 25.2 us
  between operations: 14.4 us -> 0.86 us
  local copies, waits for them, and re-layouts: 12.5 us -> 25.9 us
  blocking collectives: 20.2 us -> 27.4 us
  other arithmetic: 5.5 us -> 11 us
    all_gather x2 -> x0, waiting for transfers between devices: 203 us -> none  [circ_carry(): piece = lax.all_gather(state[None], 'circ', axis=0, tiled=True)]
    all_to_all x0 -> x2, waiting for transfers between devices: none -> 83.7 us  [circ_carry(): lax.all_to_all(jnp.stack([state[None]] * lax.axis_size('circ')), 'circ',...]
    all_to_all x0 -> x2, starting transfers between devices: none -> 19.7 us  [circ_carry(): lax.all_to_all(jnp.stack([state[None]] * lax.axis_size('circ')), 'circ',...]
    all_gather x2, blocking collectives: 13.9 us -> 19.1 us  [entering_2(): gathered = jax.tree.map(lambda a: lax.all_gather(a, axis), part)]
    another operation x2 -> x4, local copies, waits for them, and re-layouts: 0.01 us -> 4.05 us  [the longest x2 4.05 us: circ_carry(): jnp.stack([state[None]] * lax.axis_size('circ'))]
    dot_general x2, matrix products: 10.2 us -> 6.57 us  [circ_carry(): jnp.einsum('qs,qsfna->sfna', weights, piece, precision=PRECISE)]
  transfers between devices with their start and end apart: 6 -> 6, of which waited for: 4 -> 4; matrix products, arithmetic and copies ran while one was open for 5% -> 15% of each run, Pallas kernels for 0% -> 0%
where the time goes in v1:
time: 200 us; the launch traced here: 199 us
  waiting for transfers between devices  96.4 us (48%)
  blocking collectives  27.4 us (14%)
  local copies, waits for them, and re-layouts  25.9 us (13%)
  starting transfers between devices  25.2 us (13%)
  matrix products  12.2 us (6%)
  other arithmetic  11 us (6%)
    all_to_all x2, waiting for transfers between devices, circ_carry(): lax.all_to_all(jnp.stack([state[None]] * lax.axis_size('circ')), 'circ',...  83.7 us
    all_to_all x2, starting transfers between devices, circ_carry(): lax.all_to_all(jnp.stack([state[None]] * lax.axis_size('circ')), 'circ',...  19.7 us
    all_gather x2, blocking collectives, entering_2(): gathered = jax.tree.map(lambda a: lax.all_gather(a, axis), part)  19.1 us
    ppermute x2, waiting for transfers between devices, with_halo(): before = lax.ppermute(last, axis, up)  9.18 us
    unnamed x1, blocking collectives  8.29 us
    unnamed x22, local copies, waits for them, and re-layouts  6.61 us
    dot_general x2, matrix products, circ_carry(): jnp.einsum('qs,qsfna->sfna', weights, piece, precision=PRECISE)  6.57 us
    add x3, other arithmetic, affine_chain(): return (earlier[0] * later[0], later[0] * earlier[1] + later[1])  4.07 us
  transfers between devices with their start and end apart: 6, of which 4 were waited for; matrix products, arithmetic and copies ran while one was open for 15% of the time, Pallas kernels for 0%

profile of v1, /device:TPU:2, one launch (start us, length us, event | category | flops | bytes accessed | tf_op | source)
XLA Modules:
  0.0 198.9 jit_solution(6882027297634672441)
XLA Ops:
  1.7 2.3 %collective-permute-start = (f32[3,8,5,256]{3,2,1,0:T(8,128)S(1)}, f32[3,8,5,256]{3,2,1,0:T(8,128)S(1)}, u32[]{:S(2)}, u32[]{:S(2)}) collective-permute-start(f32[3,8,5,256]{3,2,1,0:T(8,128)S(1)} %get-tuple-element.162), channel_id=1, source_target_pairs={{4,0},{8,4},{12,8},{16,12},{20,16},{24,20},{28,24},{32,28},{36,32}... | collective-permute-start | bytes 368648 | tf_op jit(solution)/shard_map/ppermute | solution.py:23
  5.0 3.4 %collective-permute-done = f32[3,8,5,256]{3,2,1,0:T(8,128)S(1)} collective-permute-done((f32[3,8,5,256]{3,2,1,0:T(8,128)S(1)}, f32[3,8,5,256]{3,2,1,0:T(8,128)S(1)}, u32[]{:S(2)}, u32[]{:S(2)}) %collective-permute-start) | collective-permute-done | bytes 122912 | tf_op jit(solution)/shard_map/ppermute | solution.py:23
  8.4 9.2 %collective-permute-done.1 = f32[3,8,5,256]{3,2,1,0:T(8,128)S(1)} collective-permute-done((f32[3,8,5,256]{3,2,1,0:T(8,128)S(1)}, f32[3,8,5,256]{3,2,1,0:T(8,128)S(1)}, u32[]{:S(2)}, u32[]{:S(2)}) %collective-permute-start.1) | collective-permute-done | bytes 122912 | tf_op jit(solution)/shard_map/ppermute | solution.py:22
  17.6 3.1 %multiply_bitcast_fusion = (f32[1,3,8,8,256]{4,3,2,1,0:T(8,128)S(1)}, f32[1,3,8,8,256]{4,3,2,1,0:T(8,128)S(1)}, f32[3,8,8,258]{3,2,1,0:T(8,128)}) fusion(f32[3,8,13,256]{3,2,1,0:T(8,128)S(1)} %constant_dynamic-update-slice_fusion, f32[3,8,8,256]{3,2,1,0:T(8,128)} %param.16, f32[3,8,5,256]{3,2,1,0:T(8,128)S(1)} %collective-permute-done.1), kind=kLoop, calls=%fused_computation.79 | loop fusion | flops 1474559 | bytes 1892352 | tf_op jit(solution)/shard_map/stack | solution.py:169
  21.3 2.0 %stack.18 = f32[64,1,2,3,8,256]{5,4,3,2,1,0:T(8,128)} broadcast(f32[2,3,8,256]{3,2,1,0:T(8,128)S(1)} %bitcast.88), dimensions={2,3,4,5} | broadcast | bytes 3194880 | tf_op jit(solution)/shard_map/stack | solution.py:195
  23.3 11.6 %all-to-all-start = ((f32[64,1,2,3,8,256]{5,4,3,2,1,0:T(8,128)}), f32[64,1,2,3,8,256]{5,4,3,2,1,0:T(8,128)S(1)}, u32[]{:S(2)}, u32[]{:S(2)}) async-start(f32[64,1,2,3,8,256]{5,4,3,2,1,0:T(8,128)} %stack.18), calls=%async_computation | async-start | bytes 6291456 | tf_op jit(solution)/shard_map/all_to_all | solution.py:195
  35.8 71.7 %all-to-all-done = f32[64,1,2,3,8,256]{5,4,3,2,1,0:T(8,128)S(1)} async-done(((f32[64,1,2,3,8,256]{5,4,3,2,1,0:T(8,128)}), f32[64,1,2,3,8,256]{5,4,3,2,1,0:T(8,128)S(1)}, u32[]{:S(2)}, u32[]{:S(2)}) %all-to-all-start) | async-done | bytes 3145760 | tf_op jit(solution)/shard_map/all_to_all | solution.py:195
  107.5 3.3 %fusion.2 = f32[2,1,3,8,256]{4,1,3,2,0:T(1,128)S(1)} fusion(f32[64,2,1,1,1]{0,2,4,3,1:T(1,128)S(1)} %bitcast.91, f32[64,2,3,8,256]{4,3,2,1,0:T(8,128)S(1)} %bitcast.83), kind=kOutput, calls=%fused_computation.6 | convolution fusion | flops 9437184 | bytes 3195392 | tf_op jit(solution)/shard_map/qs,qsfna->sfna/dot_general | solution.py:203
  112.1 2.0 %stack.19 = f32[64,1,2,3,8,256]{5,4,3,2,1,0:T(8,128)} broadcast(f32[2,3,8,256]{3,2,1,0:T(8,128)S(1)} %bitcast.89), dimensions={2,3,4,5} | broadcast | bytes 3194880 | tf_op jit(solution)/shard_map/stack | solution.py:195
  114.1 8.1 %all-to-all-start.1 = ((f32[64,1,2,3,8,256]{5,4,3,2,1,0:T(8,128)}), f32[64,1,2,3,8,256]{5,4,3,2,1,0:T(8,128)S(1)}, u32[]{:S(2)}, u32[]{:S(2)}) async-start(f32[64,1,2,3,8,256]{5,4,3,2,1,0:T(8,128)} %stack.19), calls=%async_computation.1 | async-start | bytes 6291456 | tf_op jit(solution)/shard_map/all_to_all | solution.py:195
  122.9 1.9 collective-permute-start.2
  128.4 2.4 %bitcast_dynamic-update-slice_fusion.1 = f32[4]{0:T(128)} fusion(f32[4]{0:T(128)} %broadcast.228.clone, u32[]{:T(128)} %bitcast.26, f32[1,1]{1,0:T(1,128)} %dynamic-slice.2), kind=kLoop, calls=%fused_computation.138 | loop fusion | bytes 1040
  130.9 1.4 bitcast_dynamic-update-slice_fusion
  135.4 8.3 %all-reduce.2 = (f32[4]{0:T(128)}, f32[4]{0:T(128)}) all-reduce(f32[4]{0:T(128)} %bitcast_dynamic-update-slice_fusion.1, f32[4]{0:T(128)S(1)} %bitcast_dynamic-update-slice_fusion), channel_id=2, replica_groups=mesh['circ'=64,'ax'=4] {'ax'}, use_global_device_ids=true, to_apply=%add | all-reduce | flops 8 | bytes 64
  144.3 1.8 fusion.11
  148.6 5.7 %all-gather.1 = f32[12,8,8,1]{2,1,3,0:T(8,128)} all-gather(f32[3,8,8,1]{2,1,3,0:T(8,128)S(1)} %copy.17), channel_id=3, replica_groups=mesh['circ'=64,'ax'=4] {'ax'}, dimensions={0}, use_global_device_ids=true | all-gather | bytes 3840 | tf_op jit(solution)/shard_map/all_gather | solution.py:32
  154.3 2.2 %fusion.9 = f32[3,8,8,256]{3,2,1,0:T(8,128)} fusion(f32[4,256,256]{2,1,0:T(8,128)} %constant.190.clone, s32[]{:T(128)S(6)} %select_n.84, f32[3,8,8,256]{3,2,1,0:T(8,128)} %copy-done.3, f32[256]{0:T(256)} %bitcast.94, f32[3,8,8]{2,1,0:T(8,128)S(1)} %get-tuple-element.131, f32[256]{0:T(256)} %bitcast.92), kind=kOutput, calls=%fused_computation.26 | convolution fusion | flops 151142400 | bytes 658180 | tf_op jit(solution)/shard_map/fnck,jk->fncj/dot_general | solution.py:239
  156.5 1.5 slice.151
  159.1 13.4 %all-gather.3 = f32[12,8,8,1]{2,1,3,0:T(8,128)} all-gather(f32[3,8,8,1]{2,1,3,0:T(8,128)S(1)} %copy.18), channel_id=5, replica_groups=mesh['circ'=64,'ax'=4] {'ax'}, dimensions={0}, use_global_device_ids=true | all-gather | bytes 3840 | tf_op jit(solution)/shard_map/all_gather | solution.py:32
  172.5 7.8 %while.27 = (s32[]{:T(128)}, f32[3,8,8]{2,1,0:T(8,128)S(1)}, s32[]{:T(128)}, f32[4,1,1,1]{0,3,2,1:T(1,128)}, f32[4,3,8,8]{3,2,1,0:T(8,128)}, /*index=5*/s32[]{:T(128)}, s32[]{:T(128)}, s32[]{:T(128)}, s32[]{:T(128)}) while((s32[]{:T(128)}, f32[3,8,8]{2,1,0:T(8,128)S(1)}, s32[]{:T(128)}, f32[4,1,1,1]{0,3,2,1:T(1,128)}, ...), condition=%wide.region_3.4_spmd, body=%wide.region_2.3_spmd.sunk | while | flops 390 | bytes 2471 | solution.py:41
  176.4 1.4 bitcast_add_fusion.5
  180.3 1.7 multiply_add_fusion.1
  182.0 12.0 %all-to-all-done.1 = f32[64,1,2,3,8,256]{5,4,3,2,1,0:T(8,128)S(1)} async-done(((f32[64,1,2,3,8,256]{5,4,3,2,1,0:T(8,128)}), f32[64,1,2,3,8,256]{5,4,3,2,1,0:T(8,128)S(1)}, u32[]{:S(2)}, u32[]{:S(2)}) %all-to-all-start.1) | async-done | bytes 3145760 | tf_op jit(solution)/shard_map/all_to_all | solution.py:195
  194.1 3.3 %fusion = f32[2,1,3,8,256]{4,1,3,2,0:T(1,128)S(1)} fusion(f32[64,2,1,1,1]{0,2,4,3,1:T(1,128)S(1)} %bitcast.90, f32[64,2,3,8,256]{4,3,2,1,0:T(8,128)S(1)} %bitcast.82), kind=kOutput, calls=%fused_computation.4 | convolution fusion | flops 9437184 | bytes 3195392 | tf_op jit(solution)/shard_map/qs,qsfna->sfna/dot_general | solution.py:203
  (55 shorter events, 24.2 us)
Async XLA Ops:
  0.6 20.1 %copy-start.5 = (f32[2,8,8,1,1]{2,1,4,3,0:T(8,128)S(1)}, f32[2,8,8,1,1]{2,1,4,3,0:T(8,128)}, u32[]{:S(2)}) copy-start(f32[2,8,8,1,1]{2,1,4,3,0:T(8,128)} %constant.206) | copy-start | bytes 1540
  1.7 6.7 %collective-permute-start = (f32[3,8,5,256]{3,2,1,0:T(8,128)S(1)}, f32[3,8,5,256]{3,2,1,0:T(8,128)S(1)}, u32[]{:S(2)}, u32[]{:S(2)}) collective-permute-start(f32[3,8,5,256]{3,2,1,0:T(8,128)S(1)} %get-tuple-element.162), channel_id=1, source_target_pairs={{4,0},{8,4},{12,8},{16,12},{20,16},{24,20},{28,24},{32,28},{36,32}... | collective-permute-start | bytes 368648 | tf_op jit(solution)/shard_map/ppermute | solution.py:23
  4.0 13.6 %collective-permute-start.1 = (f32[3,8,5,256]{3,2,1,0:T(8,128)S(1)}, f32[3,8,5,256]{3,2,1,0:T(8,128)S(1)}, u32[]{:S(2)}, u32[]{:S(2)}) collective-permute-start(f32[3,8,5,256]{3,2,1,0:T(8,128)S(1)} %get-tuple-element.163), channel_id=1, source_target_pairs={{0,4},{4,8},{8,12},{12,16},{16,20},{20,24},{24,28},{28,32},{32,36}... | collective-permute-start | bytes 368648 | tf_op jit(solution)/shard_map/ppermute | solution.py:22
  23.3 84.2 %all-to-all-start = ((f32[64,1,2,3,8,256]{5,4,3,2,1,0:T(8,128)}), f32[64,1,2,3,8,256]{5,4,3,2,1,0:T(8,128)S(1)}, u32[]{:S(2)}, u32[]{:S(2)}) async-start(f32[64,1,2,3,8,256]{5,4,3,2,1,0:T(8,128)} %stack.18), calls=%async_computation | async-start | bytes 6291456 | tf_op jit(solution)/shard_map/all_to_all | solution.py:195
  34.9 75.8 %copy-start.4 = (f32[2,8,8,1,1]{2,1,4,3,0:T(8,128)S(1)}, f32[2,8,8,1,1]{2,1,4,3,0:T(8,128)}, u32[]{:S(2)}) copy-start(f32[2,8,8,1,1]{2,1,4,3,0:T(8,128)} %constant.207) | copy-start | bytes 1540
  112.0 2.1 %copy-start.1 = (f32[2,3,8,8,256]{4,3,2,1,0:T(8,128)}, f32[2,3,8,8,256]{4,3,2,1,0:T(8,128)S(1)}, u32[]{:S(2)}) copy-start(f32[2,3,8,8,256]{4,3,2,1,0:T(8,128)S(1)} %convolution_bitcast_fusion) | copy-start | bytes 1179652
  114.1 8.1 %copy-start = (f32[3,8,8,256]{3,2,1,0:T(8,128)S(1)}, f32[3,8,8,256]{3,2,1,0:T(8,128)}, u32[]{:S(2)}) copy-start(f32[3,8,8,256]{3,2,1,0:T(8,128)} %param.16) | copy-start | bytes 589828
  114.1 12.0 %copy-start.6 = (u32[256]{0:T(256)S(1)}, u32[256]{0:T(256)}, u32[]{:S(2)}) copy-start(u32[256]{0:T(256)} %constant.196) | copy-start | bytes 3076
  114.1 80.0 %all-to-all-start.1 = ((f32[64,1,2,3,8,256]{5,4,3,2,1,0:T(8,128)}), f32[64,1,2,3,8,256]{5,4,3,2,1,0:T(8,128)S(1)}, u32[]{:S(2)}, u32[]{:S(2)}) async-start(f32[64,1,2,3,8,256]{5,4,3,2,1,0:T(8,128)} %stack.19), calls=%async_computation.1 | async-start | bytes 6291456 | tf_op jit(solution)/shard_map/all_to_all | solution.py:195
  122.9 21.4 %collective-permute-start.2 = (f32[3,8,8,2]{3,2,1,0:T(8,128)S(1)}, f32[3,8,8,2]{3,2,1,0:T(8,128)}, u32[]{:S(2)}, u32[]{:S(2)}) collective-permute-start(f32[3,8,8,2]{3,2,1,0:T(8,128)S(1)} %get-tuple-element.159), channel_id=1, source_target_pairs={{0,1},{1,2},{2,3},{4,5},{5,6},{6,7},{8,9},{9,10},{10,11},{12,13},{... | collective-permute-start | bytes 4616 | tf_op jit(solution)/shard_map/ppermute | solution.py:22
  124.8 18.9 %collective-permute-start.3 = (f32[3,8,8,2]{3,2,1,0:T(8,128)}, f32[3,8,8,2]{3,2,1,0:T(8,128)S(1)}, u32[]{:S(2)}, u32[]{:S(2)}) collective-permute-start(f32[3,8,8,2]{3,2,1,0:T(8,128)} %get-tuple-element.160), channel_id=1, source_target_pairs={{1,0},{2,1},{3,2},{5,4},{6,5},{7,6},{9,8},{10,9},{11,10},{13,12},{... | collective-permute-start | bytes 4616 | tf_op jit(solution)/shard_map/ppermute | solution.py:23
  146.1 0.7 copy-start.3
  146.8 50.6 %copy-start.2 = (f32[2,3,8,8,256]{4,3,2,1,0:T(8,128)S(1)}, f32[2,3,8,8,256]{4,3,2,1,0:T(8,128)}, u32[]{:S(2)}) copy-start(f32[2,3,8,8,256]{4,3,2,1,0:T(8,128)} %copy-done.1) | copy-start | bytes 1179652
